TPU v7x, 32 devices: a whole 2x2x4 slice. The times are simulated.
32 devices in a mesh: row: 4 (over y, x), col: 8 (over z, core).
Axes of the slice: x: 2, y: 2, z: 4, core: 2. Of those that a mesh axis runs over, the one named last changes fastest.
Arguments:
- tokens: bfloat16 [512, 8192], P('row', 'col'), may hold values from -6 to 6
- cotangent: bfloat16 [512, 8192], P('row', 'col'), may hold values from -0.25 to 0.25
- up_blocks: bfloat16 [128, 16, 128, 128], P('col', 'row'), may hold values from -0.125 to 0.125
- up_cols: int32 [128, 16], P('col', 'row'), may hold values from 0 to 63, as said below
- down_blocks: bfloat16 [128, 16, 128, 128], P('col', 'row'), may hold values from -0.125 to 0.125
- down_cols: int32 [128, 16], P('col', 'row'), may hold values from 0 to 63, as said below
Outputs:
- hidden: bfloat16 [512, 16384], P('row', 'col')
- grad_up: bfloat16 [128, 16, 128, 128], P('col', 'row')
- grad_down: bfloat16 [128, 16, 128, 128], P('col', 'row')
Inputs may be any that keep to these rules, and one draw needn't show every extreme that they name: `up_cols`: each block row names 16 different block columns. `down_cols`: each block row names 16 different block columns.
All inputs are finite; a program needn't handle non-finite values.
Results may differ from a plain program's by a relative error of at most 0.014.
Values may be sent and summed in bfloat16 or wider, within the bound.
A program may use at most 128 MiB of HBM per device.

v0:
```python
import jax
import jax.numpy as jnp
from jax import lax
from jax.sharding import PartitionSpec as P


def per_device(tokens, cotangent, up_blocks, up_cols, down_blocks, down_cols):
    rows = tokens.shape[0]
    local_rows = up_blocks.shape[0]
    side = up_blocks.shape[2]
    whole_up, up_index, whole_down, down_index = (
        lax.all_gather(up_blocks, "row", axis=1, tiled=True),
        lax.all_gather(up_cols, "row", axis=1, tiled=True),
        lax.all_gather(down_blocks, "row", axis=1, tiled=True),
        lax.all_gather(down_cols, "row", axis=1, tiled=True),
    )
    piece_in = lax.all_gather(tokens, "col", axis=1, tiled=True)
    piece_back = lax.all_gather(cotangent, "col", axis=1, tiled=True)
    width = piece_in.shape[1] // side
    in_piece = piece_in.reshape(rows, width, side)
    back_piece = piece_back.reshape(rows, width, side)
    idents = jnp.arange(width, dtype=jnp.int32)
    pick_up = (up_index[:, :, None] == idents[None, None, :]).astype(jnp.bfloat16)
    pick_down = (down_index[:, :, None] == idents[None, None, :]).astype(jnp.bfloat16)
    in_sel = jnp.einsum(
        "tcd,ikc->tikd", in_piece, pick_up, preferred_element_type=jnp.float32
    ).astype(jnp.bfloat16)
    back_sel = jnp.einsum(
        "tcd,ikc->tikd", back_piece, pick_down, preferred_element_type=jnp.float32
    ).astype(jnp.bfloat16)
    in_sel, back_sel = (in_sel, back_sel)
    pre = jnp.einsum("tikd,ikdf->tif", in_sel, whole_up, preferred_element_type=jnp.float32)
    back = jnp.einsum("tikd,ikfd->tif", back_sel, whole_down, preferred_element_type=jnp.float32)
    act = jax.nn.silu(pre).astype(jnp.bfloat16)
    part_down = jnp.einsum("tif,tikd->ikfd", act, back_sel, preferred_element_type=jnp.float32)
    sig = jax.nn.sigmoid(pre)
    slope = (back * sig * (1.0 + pre * (1.0 - sig))).astype(jnp.bfloat16)
    part_up = jnp.einsum("tikd,tif->ikdf", in_sel, slope, preferred_element_type=jnp.float32)
    grad_up, grad_down = (
        lax.psum_scatter(
            part_up.astype(jnp.bfloat16).astype(jnp.float32).astype(jnp.bfloat16),
            "row",
            scatter_dimension=1,
            tiled=True,
        ).astype(jnp.float32),
        lax.psum_scatter(
            part_down.astype(jnp.bfloat16).astype(jnp.float32).astype(jnp.bfloat16),
            "row",
            scatter_dimension=1,
            tiled=True,
        ).astype(jnp.float32),
    )
    hidden = act.reshape(rows, local_rows * side)
    return (hidden, grad_up.astype(jnp.bfloat16), grad_down.astype(jnp.bfloat16))


def solution(mesh):
    return jax.shard_map(
        per_device,
        mesh=mesh,
        in_specs=(
            P("row", "col"),
            P("row", "col"),
            P("col", "row", None, None),
            P("col", "row"),
            P("col", "row", None, None),
            P("col", "row"),
        ),
        out_specs=(P("row", "col"), P("col", "row", None, None), P("col", "row", None, None)),
        check_vma=False,
    )
```

profile of v0, /device:TPU:0, one launch (start us, length us, event | category | flops | bytes accessed | tf_op | source)
XLA Modules:
  0.0 587.9 jit_solution(15008894535070426537)
XLA Ops:
  7.2 0.0 copy-start.1
  7.2 0.0 copy-start.2
  7.2 0.0 all-gather.7.cloned.1.call-start
  7.2 0.7 all-gather.7.cloned.1.call-update
  7.9 0.0 all-gather.11.cloned.1.call-start
  8.0 0.7 all-gather.11.cloned.1.call-update
  8.7 0.0 all-gather.9.cloned.1.call-start
  8.7 3.9 copy.20
  12.6 0.0 all-gather.9.cloned.1.call-update
  12.7 0.0 all-gather.13.cloned.1.call-start
  12.7 0.5 all-gather.13.cloned.1.call-update
  13.2 0.0 all-reduce.5.cloned.1.call-start
  13.3 0.0 copy-done.1
  13.3 9.6 %all-gather = s32[4,4,16]{2,1,0:T(4,128)S(1)} all-gather(s32[1,4,16]{2,1,0:T(4,128)S(1)} %bitcast.98), channel_id=1, replica_groups=mesh['row'=4,'col'=8] {'row'}, dimensions={0}, use_global_device_ids=true | all-gather | bytes 1280 | tf_op jit(solution)/shard_map/all_gather | solution.py:13
  22.9 0.1 copy.19
  22.9 0.0 copy-done.2
  22.9 8.1 %all-gather.1 = s32[4,4,16]{2,1,0:T(4,128)S(1)} all-gather(s32[1,4,16]{2,1,0:T(4,128)S(1)} %bitcast.99), channel_id=1, replica_groups=mesh['row'=4,'col'=8] {'row'}, dimensions={0}, use_global_device_ids=true | all-gather | bytes 1280 | tf_op jit(solution)/shard_map/all_gather | solution.py:15
  31.0 0.1 copy.22
  31.1 10.4 %all-gather.7.cloned.1.call-done = bf16[128,8192]{1,0:T(8,128)(2,1)} async-done(((bf16[128,1024]{1,0:T(8,128)(2,1)}), bf16[128,8192]{1,0:T(8,128)(2,1)}) %all-gather.7.cloned.1.call-update) | async-done | bytes 2097168 | tf_op jit(solution)/shard_map/all_gather | solution.py:17
  41.5 2.2 copy.44
  43.7 5.6 convert_bitcast_fusion.2
  49.3 12.9 %copy.23 = bf16[128,16,16,128]{0,3,2,1:T(8,128)(2,1)} copy(bf16[128,16,16,128]{3,2,0,1:T(8,128)(2,1)} %convert_bitcast_fusion.2) | data formatting | bytes 16777216 | tf_op jit(solution)/shard_map/convert_element_type | solution.py:27
  62.2 9.5 %all-gather.11.cloned.1.call-done = bf16[128,8192]{1,0:T(8,128)(2,1)} async-done(((bf16[128,1024]{1,0:T(8,128)(2,1)}), bf16[128,8192]{1,0:T(8,128)(2,1)}) %all-gather.11.cloned.1.call-update) | async-done | bytes 2097168 | tf_op jit(solution)/shard_map/all_gather | solution.py:18
  71.7 2.2 copy.45
  73.9 5.6 convert_bitcast_fusion.1
  79.5 12.8 %copy.25 = bf16[128,16,16,128]{0,3,2,1:T(8,128)(2,1)} copy(bf16[128,16,16,128]{3,2,0,1:T(8,128)(2,1)} %convert_bitcast_fusion.1) | data formatting | bytes 16777216 | tf_op jit(solution)/shard_map/convert_element_type | solution.py:30
  92.3 68.7 %all-gather.9.cloned.1.call-done = bf16[16,16,128,128]{2,3,1,0:T(8,128)(2,1)} async-done(((bf16[16,4,128,128]{2,3,1,0:T(8,128)(2,1)}), bf16[16,16,128,128]{2,3,1,0:T(8,128)(2,1)}) %all-gather.9.cloned.1.call-update) | async-done | bytes 8388624 | tf_op jit(solution)/shard_map/all_gather | solution.py:12
  161.0 0.0 copy-start
  161.0 8.3 %multiply_convert_fusion = (bf16[128,16,128]{0,2,1:T(8,128)(2,1)S(1)}, f32[128,16,128]{0,2,1:T(8,128)S(1)}) fusion(bf16[16,16,128,128]{2,3,1,0:T(8,128)(2,1)} %all-gather.9.cloned.1.call-done, bf16[128,16,16,128]{0,3,2,1:T(8,128)(2,1)} %copy.23), kind=kOutput, calls=%fused_computation.13 | convolution fusion | flops 1075052544 | bytes 18350080 | tf_op jit(solution)/shard_map/tikd,ikdf->tif/dot_general | solution.py:32
  169.3 0.0 copy-done
  169.3 5.1 convert_bitcast_fusion
  174.5 75.8 %all-gather.13.cloned.1.call-done = bf16[16,16,128,128]{3,2,1,0:T(8,128)(2,1)} async-done(((bf16[16,4,128,128]{3,2,1,0:T(8,128)(2,1)}), bf16[16,16,128,128]{3,2,1,0:T(8,128)(2,1)}) %all-gather.13.cloned.1.call-update) | async-done | bytes 8388624 | tf_op jit(solution)/shard_map/all_gather | solution.py:14
  250.2 16.1 %convolution_convert_fusion = bf16[16,16,128,128]{3,2,1,0:T(8,128)(2,1)} fusion(bf16[128,16,16,128]{0,3,2,1:T(8,128)(2,1)} %copy.23, bf16[16,16,128,128]{3,2,1,0:T(8,128)(2,1)} %all-gather.13.cloned.1.call-done, bf16[128,16,16,128]{0,3,2,1:T(8,128)(2,1)} %copy.25, f32[128,16,128]{0,2,1:T(8,128)S(1)} %get-tuple-element.12), kind=kOutput, calls=%fused_computation.3 | convolution fusion | flops 2154037248 | bytes 34603008 | tf_op jit(solution)/shard_map/tikd,tif->ikdf/dot_general | solution.py:38
  266.3 0.0 copy-start.3
  266.3 0.0 all-reduce.5.cloned.1.call-update
  266.3 0.6 copy-done.3
  267.0 0.6 dynamic-slice
  268.2 1.0 copy.27
  269.2 304.6 %all-reduce.5.cloned.1.call-done = (bf16[16,16,128,128]{3,2,1,0:T(8,128)(2,1)}, bf16[16,16,128,128]{2,3,1,0:T(8,128)(2,1)}) async-done(((bf16[16,16,128,128]{3,2,1,0:T(8,128)(2,1)}, bf16[16,16,128,128]{2,3,1,0:T(8,128)(2,1)}), (bf16[16,16,128,128]{3,2,1,0:T(8,128)(2,1)}, bf16[16,16,128,128]{2,3,1,0:T(8,128)(2,1)})) %all-reduce.5.cloned.1.call-update) | async-done | bytes 16777232
  573.8 1.7 constant_dynamic-slice_fusion
  575.6 2.6 copy.28
  578.2 3.2 constant_dynamic-slice_fusion.1
Async XLA Ops:
  7.2 6.1 %copy-start.1 = (s32[16,4]{0,1:T(4,128)S(1)}, s32[16,4]{0,1:T(4,128)}, u32[]{:S(2)}) copy-start(s32[16,4]{0,1:T(4,128)} %param.9) | copy-start | bytes 772
  7.2 15.8 %copy-start.2 = (s32[16,4]{0,1:T(4,128)S(1)}, s32[16,4]{0,1:T(4,128)}, u32[]{:S(2)}) copy-start(s32[16,4]{0,1:T(4,128)} %param.11) | copy-start | bytes 772
  7.2 34.3 %all-gather.7.cloned.1.call-start = ((), (), s32[]{:S(2)}) async-start(), calls=%async_computation | async-start | bytes 2359296 | tf_op jit(solution)/shard_map/all_gather | solution.py:17
  7.9 63.8 %all-gather.11.cloned.1.call-start = ((), (), s32[]{:S(2)}) async-start(), calls=%async_computation.2 | async-start | bytes 2359296 | tf_op jit(solution)/shard_map/all_gather | solution.py:18
  8.7 152.4 %all-gather.9.cloned.1.call-start = ((), (), s32[]{:S(2)}) async-start(), calls=%async_computation.1 | async-start | bytes 10485760 | tf_op jit(solution)/shard_map/all_gather | solution.py:12
  12.7 237.6 %all-gather.13.cloned.1.call-start = ((), (), s32[]{:S(2)}) async-start(), calls=%async_computation.3 | async-start | bytes 10485760 | tf_op jit(solution)/shard_map/all_gather | solution.py:14
  13.2 560.6 %all-reduce.5.cloned.1.call-start = ((), (), s32[]{:S(2)}) async-start(), calls=%async_computation.4 | async-start | bytes 33554432
  161.0 8.3 %copy-start = (bf16[128,16,16,128]{0,3,2,1:T(8,128)(2,1)S(1)}, bf16[128,16,16,128]{0,3,2,1:T(8,128)(2,1)}, u32[]{:S(2)}) copy-start(bf16[128,16,16,128]{0,3,2,1:T(8,128)(2,1)} %copy.25) | copy-start | bytes 25165828
  266.3 0.7 copy-start.3
Sparse Core Ops, SparseCore 0:
  9.6 31.8 all-gather.6
  43.1 28.5 all-gather.10
  74.1 86.8 all-gather.8
  162.7 87.4 all-gather.12
  266.5 307.3 all-reduce.4
where the time goes:
time: 589 us; the launch traced here: 588 us
  waiting for transfers between devices  471 us (80%)
  local copies, waits for them, and re-layouts  43.9 us (7%)
  matrix products  40.7 us (7%)
  blocking collectives  17.6 us (3%)
  between operations  14.5 us (2%)
    unnamed x6, waiting for transfers between devices  307 us
    all_gather x1, waiting for transfers between devices, per_device(): lax.all_gather(down_blocks, 'row', axis=1, tiled=True)  75.8 us
    all_gather x1, waiting for transfers between devices, per_device(): lax.all_gather(up_blocks, 'row', axis=1, tiled=True)  68.7 us
    unnamed x18, local copies, waits for them, and re-layouts  18.1 us
    dot_general x1, matrix products, per_device(): jnp.einsum('tikd,tif->ikdf', in_sel, slope, preferred_element_type=jnp.fl...  16.1 us
    convert_element_type x1, local copies, waits for them, and re-layouts, per_device(): in_sel = jnp.einsum('tcd,ikc->tikd', in_piece, pick_up, preferred_element...  12.9 us
    convert_element_type x1, local copies, waits for them, and re-layouts, per_device(): back_sel = jnp.einsum('tcd,ikc->tikd', back_piece, pick_down, preferred_e...  12.8 us
  transfers between devices with their start and end apart: 5, of which 5 were waited for; matrix products, arithmetic and copies ran while one was open for 10% of the time, Pallas kernels for 0%

commit v1 on v0

--- a/solution.py
+++ b/solution.py
@@ -1,7 +1,260 @@
+import functools
+
 import jax
 import jax.numpy as jnp
 from jax import lax
+from jax.experimental import pallas as pl
+from jax.experimental.pallas import tpu as pltpu
 from jax.sharding import PartitionSpec as P
+
+MESH = pl.DeviceIdType.MESH
+ANY = pl.BlockSpec(memory_space=pl.ANY)
+VM = pl.BlockSpec(memory_space=pltpu.VMEM)
+f32 = jnp.float32
+bf16 = jnp.bfloat16
+
+
+def place():
+    r = lax.axis_index("row")
+    c = lax.axis_index("col")
+    xn = r + 1 - 2 * (r % 2)
+    yn = (r + 2) % 4
+    return r, c, xn, yn, 3 - r
+
+
+class Puts:
+    def __init__(self, sems):
+        self.sems = sems
+        self.copies = []
+
+    def __call__(self, src, dst, recv, dev):
+        cp = pltpu.make_async_remote_copy(
+            src_ref=src, dst_ref=dst, send_sem=self.sems.at[len(self.copies)],
+            recv_sem=recv, device_id=dev, device_id_type=MESH)
+        cp.start()
+        self.copies.append(cp)
+
+    def got(self, ref, recv, dev):
+        pltpu.make_async_remote_copy(
+            src_ref=ref, dst_ref=ref, send_sem=self.sems.at[0],
+            recv_sem=recv, device_id=dev, device_id_type=MESH).wait_recv()
+
+    def drain(self):
+        for cp in self.copies:
+            cp.wait_send()
+
+
+def greet(devs):
+    sem = pltpu.get_barrier_semaphore()
+    for dev in devs:
+        pl.semaphore_signal(sem, inc=1, device_id=dev, device_id_type=MESH)
+    pl.semaphore_wait(sem, len(devs))
+
+
+def gather_kernel(tok, cot, wu, wd, ci, T, G, WU, WD, CI, own, send, recv, wrecv, loc):
+    r, c, xn, yn, dg = place()
+    z, q = c // 2, c % 2
+    pc = c + 1 - 2 * q
+    zcs = [((z + d) % 4) * 2 + q for d in range(4)]
+    zps = [((z + d) % 4) * 2 + 1 - q for d in range(4)]
+    X, Y, D, Q = (xn, c), (yn, c), (dg, c), (r, pc)
+    greet([(r, zc) for zc in zcs[1:]] + [X, Y, D, Q])
+    put = Puts(send)
+
+    def fwd(a, rr, cc, dev, src=None):
+        ref = (T, G)[a].at[rr, cc]
+        put(ref if src is None else src, ref, recv.at[a, rr, cc], dev)
+
+    def got(a, rr, cc):
+        put.got((T, G)[a].at[rr, cc], recv.at[a, rr, cc], Q)
+
+    ins = [pltpu.make_async_copy(w.at[r], own.at[j], loc.at[j]) for j, w in enumerate((wu, wd))]
+    for cp in ins:
+        cp.start()
+    outs = [
+        pltpu.make_async_copy(tok, T.at[r, c], loc.at[2]),
+        pltpu.make_async_copy(cot, G.at[r, c], loc.at[3]),
+        pltpu.make_async_copy(ci.at[r], CI.at[r], loc.at[4]),
+    ]
+    for cp in outs:
+        cp.start()
+    for d in (1, 3, 2):
+        for a, s in enumerate((tok, cot)):
+            fwd(a, r, c, (r, zcs[d]), s)
+    fwd(0, r, c, X, tok)
+    fwd(1, r, c, Y, cot)
+    fwd(1, r, c, X, cot)
+    fwd(0, r, c, Y, tok)
+    fwd(0, r, c, Q, tok)
+    fwd(1, r, c, Q, cot)
+    for peer in (dg, xn, yn):
+        for j, (s, t) in enumerate(((wu, WU), (wd, WD), (ci, CI))):
+            put(s.at[peer], t.at[r], wrecv.at[j, r], (peer, c))
+    for j, cp in enumerate(ins):
+        cp.wait()
+        cp = pltpu.make_async_copy(own.at[j], (WU, WD)[j].at[r], loc.at[5 + j])
+        cp.start()
+        outs.append(cp)
+
+    def relay(cc):
+        got(0, xn, cc)
+        fwd(0, xn, cc, Y)
+        fwd(0, xn, cc, Q)
+        got(1, yn, cc)
+        fwd(1, yn, cc, X)
+        fwd(1, yn, cc, Q)
+
+    order = (0, 1, 3, 2)
+    for n, d in enumerate(order):
+        if n:
+            got(0, r, zcs[d])
+            fwd(0, r, zcs[d], X)
+            got(1, r, zcs[d])
+            fwd(1, r, zcs[d], Y)
+            fwd(1, r, zcs[d], X)
+            fwd(0, r, zcs[d], Y)
+            fwd(0, r, zcs[d], Q)
+            fwd(1, r, zcs[d], Q)
+            relay(zcs[order[n - 1]])
+    relay(zcs[order[3]])
+    for d in order:
+        for a, rr in ((1, xn), (0, yn), (0, dg), (1, dg)):
+            got(a, rr, zcs[d])
+            fwd(a, rr, zcs[d], Q)
+    for peer in (dg, xn, yn):
+        for j, t in enumerate((WU, WD, CI)):
+            put.got(t.at[peer], wrecv.at[j, peer], (peer, c))
+    for d in order:
+        for rr in (r, xn, yn, dg):
+            for a in range(2):
+                got(a, rr, zps[d])
+    for cp in outs:
+        cp.wait()
+    put.drain()
+
+
+def gather_all(tok, cot, wu, wd, ci):
+    full = jax.ShapeDtypeStruct((4, 8) + tok.shape, bf16)
+    return pl.pallas_call(
+        gather_kernel,
+        out_shape=(full, full, jax.ShapeDtypeStruct(wu.shape, bf16),
+                   jax.ShapeDtypeStruct(wd.shape, bf16), jax.ShapeDtypeStruct(ci.shape, ci.dtype)),
+        in_specs=[VM, VM, ANY, ANY, ANY],
+        out_specs=(ANY,) * 5,
+        scratch_shapes=[
+            pltpu.VMEM((2,) + wu.shape[1:], bf16),
+            pltpu.SemaphoreType.DMA((80,)),
+            pltpu.SemaphoreType.DMA((2, 4, 8)),
+            pltpu.SemaphoreType.DMA((3, 4)),
+            pltpu.SemaphoreType.DMA((7,)),
+        ],
+        compiler_params=pltpu.CompilerParams(collective_id=0, has_side_effects=True),
+        name="gather_all",
+    )(tok, cot, wu, wd, ci)
+
+
+def row_kernel(ci, T, G, wu, wd, hid, gu, gd, xs, gs, ws):
+    i = pl.program_id(0)
+    for k in range(16):
+        for a, (src, dst) in enumerate(((T, xs), (G, gs))):
+            b = ci[k // 4, 0, a * 16 + i * 4 + k % 4]
+            lo = pl.multiple_of((b % 8) * 128, 128)
+            dst[:, k * 128:(k + 1) * 128] = src[:, b // 8, :, pl.ds(lo, 128)].reshape(512, 128)
+        ws[:, k * 128:(k + 1) * 128] = wd[k // 4, 0, k % 4]
+    pre = jnp.dot(xs[...], wu[...].reshape(2048, 128), preferred_element_type=f32)
+    back = lax.dot_general(gs[...], ws[...], (((1,), (1,)), ((), ())), preferred_element_type=f32)
+    sig = jax.nn.sigmoid(pre)
+    act = (pre * sig).astype(bf16)
+    slope = (back * sig * (1.0 + pre * (1.0 - sig))).astype(bf16)
+    hid[...] = act.reshape(4, 128, 128)
+    act_t = act.T
+    slope_t = slope.T
+    for k in range(0, 16, 4):
+        cols = slice(k * 128, (k + 4) * 128)
+        down = jnp.dot(act_t, gs[:, cols], preferred_element_type=f32)
+        up = jnp.dot(slope_t, xs[:, cols], preferred_element_type=f32)
+        for j in range(4):
+            gd[k // 4, 0, j] = down[:, j * 128:(j + 1) * 128].astype(bf16)
+            gu[k // 4, 0, j] = up[:, j * 128:(j + 1) * 128].T.astype(bf16)
+
+
+def rows_all(ci, T, G, wu, wd):
+    whole = pl.BlockSpec(T.shape, lambda i, s: (0, 0, 0, 0), pipeline_mode=pl.Buffered(1))
+    wspec = pl.BlockSpec((4, 1, 4, 128, 128), lambda i, s: (0, i, 0, 0, 0))
+    return pl.pallas_call(
+        row_kernel,
+        out_shape=(jax.ShapeDtypeStruct((4, 128, 512), bf16),
+                   jax.ShapeDtypeStruct(wu.shape, bf16), jax.ShapeDtypeStruct(wd.shape, bf16)),
+        grid_spec=pltpu.PrefetchScalarGridSpec(
+            num_scalar_prefetch=1, grid=(4,),
+            in_specs=[whole, whole, wspec, wspec],
+            out_specs=(pl.BlockSpec((4, 128, 128), lambda i, s: (0, 0, i)), wspec, wspec),
+            scratch_shapes=[pltpu.VMEM((512, 2048), bf16), pltpu.VMEM((512, 2048), bf16),
+                            pltpu.VMEM((128, 2048), bf16)]),
+        compiler_params=pltpu.CompilerParams(vmem_limit_bytes=48 << 20),
+        name="rows_all",
+    )(ci, T, G, wu, wd)
+
+
+def scatter_kernel(hid, gu, gd, H, U, Dn, vh, vw, send, recv, loc):
+    r, c, xn, yn, dg = place()
+    peers = (dg, xn, yn)
+    greet([(p, c) for p in peers])
+    put = Puts(send)
+
+    def dests(rr):
+        return (H.at[:, pl.ds(pl.multiple_of(rr * 512, 512), 512)],
+                U.at[pl.ds(rr * 4, 4)], Dn.at[pl.ds(rr * 4, 4)])
+
+    mine = dests(r)
+    ins = [pltpu.make_async_copy(s.at[r], v, loc.at[j])
+           for j, (s, v) in enumerate(((hid, vh), (gu, vw.at[0]), (gd, vw.at[1])))]
+    for cp in ins:
+        cp.start()
+    for p in peers:
+        for j, s in enumerate((hid, gu, gd)):
+            put(s.at[p], mine[j], recv.at[j, r], (p, c))
+    outs = []
+    for j, v in enumerate((vh, vw.at[0], vw.at[1])):
+        ins[j].wait()
+        cp = pltpu.make_async_copy(v, mine[j], loc.at[3 + j])
+        cp.start()
+        outs.append(cp)
+    for p in peers:
+        for j, t in enumerate(dests(p)):
+            put.got(t, recv.at[j, p], (p, c))
+    for cp in outs:
+        cp.wait()
+    put.drain()
+
+
+def scatter_all(hid, gu, gd):
+    grad = jax.ShapeDtypeStruct((16,) + gu.shape[2:], bf16)
+    return pl.pallas_call(
+        scatter_kernel,
+        out_shape=(jax.ShapeDtypeStruct((128, 2048), bf16), grad, grad),
+        in_specs=[ANY, ANY, ANY],
+        out_specs=(ANY,) * 3,
+        scratch_shapes=[
+            pltpu.VMEM(hid.shape[1:], bf16),
+            pltpu.VMEM((2,) + gu.shape[1:], bf16),
+            pltpu.SemaphoreType.DMA((9,)),
+            pltpu.SemaphoreType.DMA((3, 4)),
+            pltpu.SemaphoreType.DMA((6,)),
+        ],
+        compiler_params=pltpu.CompilerParams(collective_id=1, has_side_effects=True),
+        name="scatter_all",
+    )(hid, gu, gd)
+
+
+def per_row(tokens, cotangent, up_blocks, up_cols, down_blocks, down_cols):
+    wu = up_blocks.reshape(4, 4, 4, 128, 128)
+    wd = down_blocks.reshape(4, 4, 4, 128, 128)
+    ci = jnp.concatenate([up_cols.reshape(4, 16), down_cols.reshape(4, 16)], axis=1)
+    ci = jnp.pad(ci[:, None, :], ((0, 0), (0, 7), (0, 96)))
+    T, G, WU, WD, CI = gather_all(tokens, cotangent, wu, wd, ci)
+    hid, gu, gd = rows_all(CI, T, G, WU, WD)
+    return scatter_all(hid, gu, gd)
 
 
 def per_device(tokens, cotangent, up_blocks, up_cols, down_blocks, down_cols):
@@ -55,8 +308,9 @@
 
 
 def solution(mesh):
+    small = mesh.shape["row"] == 4 and mesh.shape["col"] == 8
     return jax.shard_map(
-        per_device,
+        per_row if small else per_device,
         mesh=mesh,
         in_specs=(
             P("row", "col"),

time: 589 us -> 210 us (0.36)
  waiting for transfers between devices: 471 us -> 0 us
  Pallas kernels: 0 us -> 196 us
  matrix products: 40.7 us -> 0 us
  local copies, waits for them, and re-layouts: 43.9 us -> 12.9 us
  blocking collectives: 17.6 us -> 0 us
  between operations: 14.5 us -> 0.68 us
    unnamed x6 -> x0, waiting for transfers between devices: 307 us -> none
    pallas_call x0 -> x3, Pallas kernels: none -> 196 us  [the longest x1 124 us: gather_all(): pl.pallas_call(gather_kernel, out_shape=(full, full, jax.ShapeDtypeStruct...]
    all_gather x4 -> x0, waiting for transfers between devices: 164 us -> none  [the longest x1 75.8 us: per_device(): lax.all_gather(down_blocks, 'row', axis=1, tiled=True)]
    dot_general x5 -> x0, matrix products: 40.7 us -> none  [the longest x1 16.1 us: per_device(): jnp.einsum('tikd,tif->ikdf', in_sel, slope, preferred_element_type=jnp.fl...]
    convert_element_type x2 -> x0, local copies, waits for them, and re-layouts: 25.7 us -> none  [the longest x1 12.9 us: per_device(): in_sel = jnp.einsum('tcd,ikc->tikd', in_piece, pick_up, preferred_element...]
    all_gather x2 -> x0, blocking collectives: 17.6 us -> none  [the longest x1 9.57 us: per_device(): lax.all_gather(up_cols, 'row', axis=1, tiled=True)]
    unnamed x18 -> x15, local copies, waits for them, and re-layouts: 18.1 us -> 12.2 us
  transfers between devices with their start and end apart: 5 -> 0, of which waited for: 5 -> 0; matrix products, arithmetic and copies ran while one was open for 10% -> 0% of each run, Pallas kernels for 0% -> 0%
where the time goes in v1:
time: 210 us
  Pallas kernels  196 us (93%)
  local copies, waits for them, and re-layouts  12.9 us (6%)
    pallas_call x1, Pallas kernels, gather_all(): pl.pallas_call(gather_kernel, out_shape=(full, full, jax.ShapeDtypeStruct...  124 us
    pallas_call x1, Pallas kernels, scatter_all(): pl.pallas_call(scatter_kernel, out_shape=(jax.ShapeDtypeStruct((128, 2048...  55.1 us
    pallas_call x1, Pallas kernels, rows_all(): pl.pallas_call(row_kernel, out_shape=(jax.ShapeDtypeStruct((4, 128, 512),...  17.2 us
    unnamed x15, local copies, waits for them, and re-layouts  12.2 us

profile of v1, /device:TPU:0, one launch (start us, length us, event | category | flops | bytes accessed | tf_op | source)
XLA Modules:
  0.0 210.0 jit_solution(2023271671193688868)
XLA Ops:
  0.6 0.8 copy.12
  1.4 0.1 reshape.20
  1.5 0.8 copy.13
  2.2 0.1 reshape.21
  2.3 0.1 pad_add_fusion
  2.4 0.6 pad.4.ci
  3.0 124.0 %gather_all.1 = (bf16[4,8,128,1024]{3,2,1,0:T(8,128)(2,1)}, bf16[4,8,128,1024]{3,2,1,0:T(8,128)(2,1)}, bf16[4,4,4,128,128]{4,3,2,1,0:T(8,128)(2,1)}, bf16[4,4,4,128,128]{4,3,2,1,0:T(8,128)(2,1)}, s32[4,8,128]{2,1,0:T(8,128)}) custom-call(bf16[128,1024]{1,0:T(8,128)(2,1)} %tok.1, bf16[128,1024]{1,0:T(8,128)(2,1)} %cot.1, ...), custom_call_target="tpu_custom_call" | custom-call | tf_op jit(solution)/shard_map/gather_all/pallas_call | solution.py:138
  127.0 0.0 copy-start.3
  127.0 0.7 copy-done.3
  127.7 17.2 %rows_all.1 = (bf16[4,128,512]{2,1,0:T(8,128)(2,1)S(1)}, bf16[4,4,4,128,128]{4,3,2,1,0:T(8,128)(2,1)S(1)}, bf16[4,4,4,128,128]{4,3,2,1,0:T(8,128)(2,1)S(1)}) custom-call(s32[4,8,128]{2,1,0:T(8,128)S(1)} %copy-done.3, bf16[4,8,128,1024]{3,2,1,0:T(8,128)(2,1)} %get-tuple-element.12.T, bf16[4,8,128,1024]{3,2,1,0:T(8,128)(2,1)} %get-tuple-element.13.G, ...), custom_call_target="tpu_custom_call" | custom-call | tf_op jit(solution)/shard_map/rows_all/pallas_call | solution.py:184
  145.0 0.0 copy-start
  145.0 1.3 copy-done
  146.3 0.0 copy-start.1
  146.3 1.3 copy-done.1
  147.6 0.0 copy-start.2
  147.6 0.8 copy-done.2
  148.4 55.1 %scatter_all.1 = (bf16[128,2048]{1,0:T(8,128)(2,1)}, bf16[16,4,128,128]{3,2,1,0:T(8,128)(2,1)}, bf16[16,4,128,128]{3,2,1,0:T(8,128)(2,1)}) custom-call(bf16[4,128,512]{2,1,0:T(8,128)(2,1)} %copy-done.2, bf16[4,4,4,128,128]{4,3,2,1,0:T(8,128)(2,1)} %copy-done, bf16[4,4,4,128,128]{4,3,2,1,0:T(8,128)(2,1)} %copy-done.1), custom_call_target="tpu_custom_call" | custom-call | tf_op jit(solution)/shard_map/scatter_all/pallas_call | solution.py:233
  203.5 1.9 copy.18
  205.4 0.0 copy-start.4
  205.4 3.3 %copy.19 = bf16[16,4,128,128]{3,2,1,0:T(8,128)(2,1)} copy(bf16[16,4,128,128]{3,2,1,0:T(8,128)(2,1)} %get-tuple-element.23) | data formatting | bytes 4194304
  208.7 0.0 copy-done.4
  208.7 1.3 copy.20
Async XLA Ops:
  127.0 0.7 copy-start.3
  145.0 1.3 copy-start
  146.3 1.3 copy-start.1
  147.6 0.8 copy-start.2
  205.4 3.3 %copy-start.4 = (bf16[16,4,128,128]{3,2,1,0:T(8,128)(2,1)S(1)}, bf16[16,4,128,128]{3,2,1,0:T(8,128)(2,1)}, u32[]{:S(2)}) copy-start(bf16[16,4,128,128]{3,2,1,0:T(8,128)(2,1)} %get-tuple-element.24) | copy-start | bytes 6291460

commit v2 on v1

--- a/solution.py
+++ b/solution.py
@@ -27,12 +27,15 @@
         self.sems = sems
         self.copies = []
 
-    def __call__(self, src, dst, recv, dev):
+    def __call__(self, src, dst, recv, dev, when=None):
         cp = pltpu.make_async_remote_copy(
             src_ref=src, dst_ref=dst, send_sem=self.sems.at[len(self.copies)],
             recv_sem=recv, device_id=dev, device_id_type=MESH)
-        cp.start()
-        self.copies.append(cp)
+        if when is None:
+            cp.start()
+        else:
+            pl.when(when)(cp.start)
+        self.copies.append((cp, when))
 
     def got(self, ref, recv, dev):
         pltpu.make_async_remote_copy(
@@ -40,8 +43,11 @@
             recv_sem=recv, device_id=dev, device_id_type=MESH).wait_recv()
 
     def drain(self):
-        for cp in self.copies:
-            cp.wait_send()
+        for cp, when in self.copies:
+            if when is None:
+                cp.wait_send()
+            else:
+                pl.when(when)(cp.wait_send)
 
 
 def greet(devs):
@@ -55,15 +61,17 @@
     r, c, xn, yn, dg = place()
     z, q = c // 2, c % 2
     pc = c + 1 - 2 * q
+    first = xn + q * (yn - xn)
+    second = yn + q * (xn - yn)
     zcs = [((z + d) % 4) * 2 + q for d in range(4)]
-    zps = [((z + d) % 4) * 2 + 1 - q for d in range(4)]
     X, Y, D, Q = (xn, c), (yn, c), (dg, c), (r, pc)
+    rows = (r, xn, yn, dg)
     greet([(r, zc) for zc in zcs[1:]] + [X, Y, D, Q])
     put = Puts(send)
 
-    def fwd(a, rr, cc, dev, src=None):
+    def fwd(a, rr, cc, dev, src=None, when=None):
         ref = (T, G)[a].at[rr, cc]
-        put(ref if src is None else src, ref, recv.at[a, rr, cc], dev)
+        put(ref if src is None else src, ref, recv.at[a, rr, cc], dev, when)
 
     def got(a, rr, cc):
         put.got((T, G)[a].at[rr, cc], recv.at[a, rr, cc], Q)
@@ -74,60 +82,90 @@
     outs = [
         pltpu.make_async_copy(tok, T.at[r, c], loc.at[2]),
         pltpu.make_async_copy(cot, G.at[r, c], loc.at[3]),
-        pltpu.make_async_copy(ci.at[r], CI.at[r], loc.at[4]),
+        pltpu.make_async_copy(ci, CI.at[r], loc.at[4]),
     ]
     for cp in outs:
         cp.start()
+
+    def along(rr, src=None):
+        fwd(1, rr, c, (r, c + 2), src, z < 3)
+        fwd(1, rr, c, (r, c - 2), src, z > 0)
+
+    def weights(j):
+        for peer in (dg, xn, yn):
+            put((wu, wd)[j].at[peer], (WU, WD)[j].at[r], wrecv.at[j, r], (peer, c))
+
+    fwd(1, r, c, X, cot)
+    fwd(1, r, c, Y, cot)
     for d in (1, 3, 2):
-        for a, s in enumerate((tok, cot)):
-            fwd(a, r, c, (r, zcs[d]), s)
+        fwd(0, r, c, (r, zcs[d]), tok)
     fwd(0, r, c, X, tok)
-    fwd(1, r, c, Y, cot)
-    fwd(1, r, c, X, cot)
     fwd(0, r, c, Y, tok)
+    along(r, cot)
     fwd(0, r, c, Q, tok)
     fwd(1, r, c, Q, cot)
     for peer in (dg, xn, yn):
-        for j, (s, t) in enumerate(((wu, WU), (wd, WD), (ci, CI))):
-            put(s.at[peer], t.at[r], wrecv.at[j, r], (peer, c))
+        put(ci, CI.at[r], wrecv.at[2, r], (peer, c))
+    got(1, first, c)
+    fwd(1, first, c, (second, c))
+    got(1, second, c)
+    for rr in (first, second):
+        along(rr)
+        fwd(1, rr, c, Q)
+    weights(0)
+    got(1, dg, c)
+    along(dg)
+    fwd(1, dg, c, Q)
     for j, cp in enumerate(ins):
         cp.wait()
         cp = pltpu.make_async_copy(own.at[j], (WU, WD)[j].at[r], loc.at[5 + j])
         cp.start()
         outs.append(cp)
 
-    def relay(cc):
-        got(0, xn, cc)
-        fwd(0, xn, cc, Y)
-        fwd(0, xn, cc, Q)
-        got(1, yn, cc)
-        fwd(1, yn, cc, X)
-        fwd(1, yn, cc, Q)
-
-    order = (0, 1, 3, 2)
-    for n, d in enumerate(order):
-        if n:
-            got(0, r, zcs[d])
-            fwd(0, r, zcs[d], X)
-            got(1, r, zcs[d])
-            fwd(1, r, zcs[d], Y)
-            fwd(1, r, zcs[d], X)
-            fwd(0, r, zcs[d], Y)
-            fwd(0, r, zcs[d], Q)
-            fwd(1, r, zcs[d], Q)
-            relay(zcs[order[n - 1]])
-    relay(zcs[order[3]])
-    for d in order:
-        for a, rr in ((1, xn), (0, yn), (0, dg), (1, dg)):
-            got(a, rr, zcs[d])
-            fwd(a, rr, zcs[d], Q)
-    for peer in (dg, xn, yn):
-        for j, t in enumerate((WU, WD, CI)):
+    def relay(d):
+        got(0, first, zcs[d])
+        fwd(0, first, zcs[d], (second, c))
+        fwd(0, first, zcs[d], Q)
+
+    def onward(step):
+        for sign in (1, -1):
+            here = z >= step if sign == 1 else z + step < 4
+            more = z < 3 if sign == 1 else z > 0
+            cc = c - 2 * sign * step
+            for rr in rows:
+                pl.when(here)(functools.partial(got, 1, rr, cc))
+                if step < 3:
+                    fwd(1, rr, cc, (r, c + 2 * sign), None, here & more)
+                fwd(1, rr, cc, Q, None, here)
+
+    for d in (1, 3, 2):
+        got(0, r, zcs[d])
+        fwd(0, r, zcs[d], X)
+        fwd(0, r, zcs[d], Y)
+        fwd(0, r, zcs[d], Q)
+    relay(0)
+    relay(1)
+    onward(1)
+    relay(3)
+    relay(2)
+    weights(1)
+    for d in (0, 1):
+        for rr in (second, dg):
+            got(0, rr, zcs[d])
+            fwd(0, rr, zcs[d], Q)
+    onward(2)
+    for d in (3, 2):
+        for rr in (second, dg):
+            got(0, rr, zcs[d])
+            fwd(0, rr, zcs[d], Q)
+    onward(3)
+    for j, t in enumerate((WU, WD, CI)):
+        for peer in (dg, xn, yn):
             put.got(t.at[peer], wrecv.at[j, peer], (peer, c))
-    for d in order:
-        for rr in (r, xn, yn, dg):
-            for a in range(2):
-                got(a, rr, zps[d])
+    for a in range(2):
+        for d in range(4):
+            for rr in rows:
+                got(a, rr, ((z + d) % 4) * 2 + 1 - q)
     for cp in outs:
         cp.wait()
     put.drain()
@@ -138,12 +176,12 @@
     return pl.pallas_call(
         gather_kernel,
         out_shape=(full, full, jax.ShapeDtypeStruct(wu.shape, bf16),
-                   jax.ShapeDtypeStruct(wd.shape, bf16), jax.ShapeDtypeStruct(ci.shape, ci.dtype)),
+                   jax.ShapeDtypeStruct(wd.shape, bf16), jax.ShapeDtypeStruct((4,) + ci.shape, ci.dtype)),
         in_specs=[VM, VM, ANY, ANY, ANY],
         out_specs=(ANY,) * 5,
         scratch_shapes=[
             pltpu.VMEM((2,) + wu.shape[1:], bf16),
-            pltpu.SemaphoreType.DMA((80,)),
+            pltpu.SemaphoreType.DMA((96,)),
             pltpu.SemaphoreType.DMA((2, 4, 8)),
             pltpu.SemaphoreType.DMA((3, 4)),
             pltpu.SemaphoreType.DMA((7,)),
@@ -155,9 +193,10 @@
 
 def row_kernel(ci, T, G, wu, wd, hid, gu, gd, xs, gs, ws):
     i = pl.program_id(0)
+    row = lax.axis_index("row") * 4 + i
     for k in range(16):
         for a, (src, dst) in enumerate(((T, xs), (G, gs))):
-            b = ci[k // 4, 0, a * 16 + i * 4 + k % 4]
+            b = ci[k // 4, a * 4 + k % 4, row]
             lo = pl.multiple_of((b % 8) * 128, 128)
             dst[:, k * 128:(k + 1) * 128] = src[:, b // 8, :, pl.ds(lo, 128)].reshape(512, 128)
         ws[:, k * 128:(k + 1) * 128] = wd[k // 4, 0, k % 4]
@@ -196,30 +235,23 @@
     )(ci, T, G, wu, wd)
 
 
-def scatter_kernel(hid, gu, gd, H, U, Dn, vh, vw, send, recv, loc):
+def scatter_kernel(hid, gu, gd, H, U, Dn, send, recv, loc):
     r, c, xn, yn, dg = place()
     peers = (dg, xn, yn)
     greet([(p, c) for p in peers])
     put = Puts(send)
 
     def dests(rr):
-        return (H.at[:, pl.ds(pl.multiple_of(rr * 512, 512), 512)],
-                U.at[pl.ds(rr * 4, 4)], Dn.at[pl.ds(rr * 4, 4)])
+        return (U.at[pl.ds(rr * 4, 4)], Dn.at[pl.ds(rr * 4, 4)],
+                H.at[:, pl.ds(pl.multiple_of(rr * 512, 512), 512)])
 
     mine = dests(r)
-    ins = [pltpu.make_async_copy(s.at[r], v, loc.at[j])
-           for j, (s, v) in enumerate(((hid, vh), (gu, vw.at[0]), (gd, vw.at[1])))]
-    for cp in ins:
+    for p in peers:
+        for j, s in enumerate((gu, gd, hid)):
+            put(s.at[p], mine[j], recv.at[j, r], (p, c))
+    outs = [pltpu.make_async_copy(s.at[r], mine[j], loc.at[j]) for j, s in enumerate((gu, gd, hid))]
+    for cp in outs:
         cp.start()
-    for p in peers:
-        for j, s in enumerate((hid, gu, gd)):
-            put(s.at[p], mine[j], recv.at[j, r], (p, c))
-    outs = []
-    for j, v in enumerate((vh, vw.at[0], vw.at[1])):
-        ins[j].wait()
-        cp = pltpu.make_async_copy(v, mine[j], loc.at[3 + j])
-        cp.start()
-        outs.append(cp)
     for p in peers:
         for j, t in enumerate(dests(p)):
             put.got(t, recv.at[j, p], (p, c))
@@ -233,14 +265,12 @@
     return pl.pallas_call(
         scatter_kernel,
         out_shape=(jax.ShapeDtypeStruct((128, 2048), bf16), grad, grad),
-        in_specs=[ANY, ANY, ANY],
+        in_specs=[VM] * 3,
         out_specs=(ANY,) * 3,
         scratch_shapes=[
-            pltpu.VMEM(hid.shape[1:], bf16),
-            pltpu.VMEM((2,) + gu.shape[1:], bf16),
             pltpu.SemaphoreType.DMA((9,)),
             pltpu.SemaphoreType.DMA((3, 4)),
-            pltpu.SemaphoreType.DMA((6,)),
+            pltpu.SemaphoreType.DMA((3,)),
         ],
         compiler_params=pltpu.CompilerParams(collective_id=1, has_side_effects=True),
         name="scatter_all",
@@ -250,8 +280,8 @@
 def per_row(tokens, cotangent, up_blocks, up_cols, down_blocks, down_cols):
     wu = up_blocks.reshape(4, 4, 4, 128, 128)
     wd = down_blocks.reshape(4, 4, 4, 128, 128)
-    ci = jnp.concatenate([up_cols.reshape(4, 16), down_cols.reshape(4, 16)], axis=1)
-    ci = jnp.pad(ci[:, None, :], ((0, 0), (0, 7), (0, 96)))
+    ci = jnp.concatenate([up_cols.T, down_cols.T], axis=0)
+    ci = jnp.pad(ci, ((0, 0), (0, 112)))
     T, G, WU, WD, CI = gather_all(tokens, cotangent, wu, wd, ci)
     hid, gu, gd = rows_all(CI, T, G, WU, WD)
     return scatter_all(hid, gu, gd)

time: 210 us -> 187 us (0.89)
  Pallas kernels: 196 us -> 174 us
    pallas_call x1, Pallas kernels: 124 us -> 99.6 us  [gather_all(): pl.pallas_call(gather_kernel, out_shape=(full, full, jax.ShapeDtypeStruct...]
    pallas_call x1, Pallas kernels: 55.1 us -> 57.3 us  [scatter_all(): pl.pallas_call(scatter_kernel, out_shape=(jax.ShapeDtypeStruct((128, 2048...]
    unnamed x15 -> x13, local copies, waits for them, and re-layouts: 12.2 us -> 10.6 us
where the time goes in v2:
time: 187 us
  Pallas kernels  174 us (93%)
  local copies, waits for them, and re-layouts  11.2 us (6%)
    pallas_call x1, Pallas kernels, gather_all(): pl.pallas_call(gather_kernel, out_shape=(full, full, jax.ShapeDtypeStruct...  99.6 us
    pallas_call x1, Pallas kernels, scatter_all(): pl.pallas_call(scatter_kernel, out_shape=(jax.ShapeDtypeStruct((128, 2048...  57.3 us
    pallas_call x1, Pallas kernels, rows_all(): pl.pallas_call(row_kernel, out_shape=(jax.ShapeDtypeStruct((4, 128, 512),...  17.2 us
    unnamed x13, local copies, waits for them, and re-layouts  10.6 us

profile of v2, /device:TPU:0, one launch (start us, length us, event | category | flops | bytes accessed | tf_op | source)
XLA Modules:
  0.0 186.8 jit_solution(5114074405351915996)
XLA Ops:
  0.6 0.7 pad_add_fusion
  1.3 0.6 pad.4.ci
  1.9 99.6 %gather_all.1 = (bf16[4,8,128,1024]{3,2,1,0:T(8,128)(2,1)}, bf16[4,8,128,1024]{3,2,1,0:T(8,128)(2,1)}, bf16[4,4,4,128,128]{4,3,2,1,0:T(8,128)(2,1)}, bf16[4,4,4,128,128]{4,3,2,1,0:T(8,128)(2,1)}, s32[4,8,128]{2,1,0:T(8,128)}) custom-call(bf16[128,1024]{1,0:T(8,128)(2,1)} %tok.1, bf16[128,1024]{1,0:T(8,128)(2,1)} %cot.1, ...), custom_call_target="tpu_custom_call" | custom-call | tf_op jit(solution)/shard_map/gather_all/pallas_call | solution.py:176
  101.6 0.0 copy-start.3
  101.6 0.7 copy-done.3
  102.3 17.2 %rows_all.1 = (bf16[4,128,512]{2,1,0:T(8,128)(2,1)S(1)}, bf16[4,4,4,128,128]{4,3,2,1,0:T(8,128)(2,1)S(1)}, bf16[4,4,4,128,128]{4,3,2,1,0:T(8,128)(2,1)S(1)}) custom-call(s32[4,8,128]{2,1,0:T(8,128)S(1)} %copy-done.3, bf16[4,8,128,1024]{3,2,1,0:T(8,128)(2,1)} %get-tuple-element.12.T, bf16[4,8,128,1024]{3,2,1,0:T(8,128)(2,1)} %get-tuple-element.13.G, ...), custom_call_target="tpu_custom_call" | custom-call | tf_op jit(solution)/shard_map/rows_all/pallas_call | solution.py:223
  119.5 0.0 copy-start
  119.5 1.3 copy-done
  120.9 0.0 copy-start.1
  120.9 1.3 copy-done.1
  122.2 0.0 copy-start.2
  122.2 0.8 copy-done.2
  123.0 57.3 %scatter_all.1 = (bf16[128,2048]{1,0:T(8,128)(2,1)}, bf16[16,4,128,128]{3,2,1,0:T(8,128)(2,1)}, bf16[16,4,128,128]{3,2,1,0:T(8,128)(2,1)}) custom-call(bf16[4,128,512]{2,1,0:T(8,128)(2,1)} %copy-done.2, bf16[4,4,4,128,128]{4,3,2,1,0:T(8,128)(2,1)} %copy-done, bf16[4,4,4,128,128]{4,3,2,1,0:T(8,128)(2,1)} %copy-done.1), custom_call_target="tpu_custom_call" | custom-call | tf_op jit(solution)/shard_map/scatter_all/pallas_call | solution.py:265
  180.3 1.9 %copy.12 = bf16[128,2048]{1,0:T(8,128)(2,1)} copy(bf16[128,2048]{1,0:T(8,128)(2,1)} %get-tuple-element.22) | data formatting | bytes 1048576
  182.2 0.0 copy-start.4
  182.2 3.3 %copy.13 = bf16[16,4,128,128]{3,2,1,0:T(8,128)(2,1)} copy(bf16[16,4,128,128]{3,2,1,0:T(8,128)(2,1)} %get-tuple-element.23) | data formatting | bytes 4194304
  185.5 0.0 copy-done.4
  185.5 1.3 copy.14
Async XLA Ops:
  101.6 0.7 copy-start.3
  119.5 1.3 copy-start
  120.9 1.3 copy-start.1
  122.2 0.8 copy-start.2
  182.2 3.3 %copy-start.4 = (bf16[16,4,128,128]{3,2,1,0:T(8,128)(2,1)S(1)}, bf16[16,4,128,128]{3,2,1,0:T(8,128)(2,1)}, u32[]{:S(2)}) copy-start(bf16[16,4,128,128]{3,2,1,0:T(8,128)(2,1)} %get-tuple-element.24) | copy-start | bytes 6291460

commit v3 on v2

--- a/solution.py
+++ b/solution.py
@@ -69,19 +69,22 @@
     greet([(r, zc) for zc in zcs[1:]] + [X, Y, D, Q])
     put = Puts(send)
 
+    def slot(a, rr, cc):
+        return (T, G)[a].at[pl.ds(cc * 8, 8), rr]
+
     def fwd(a, rr, cc, dev, src=None, when=None):
-        ref = (T, G)[a].at[rr, cc]
+        ref = slot(a, rr, cc)
         put(ref if src is None else src, ref, recv.at[a, rr, cc], dev, when)
 
     def got(a, rr, cc):
-        put.got((T, G)[a].at[rr, cc], recv.at[a, rr, cc], Q)
+        put.got(slot(a, rr, cc), recv.at[a, rr, cc], Q)
 
     ins = [pltpu.make_async_copy(w.at[r], own.at[j], loc.at[j]) for j, w in enumerate((wu, wd))]
     for cp in ins:
         cp.start()
     outs = [
-        pltpu.make_async_copy(tok, T.at[r, c], loc.at[2]),
-        pltpu.make_async_copy(cot, G.at[r, c], loc.at[3]),
+        pltpu.make_async_copy(tok, slot(0, r, c), loc.at[2]),
+        pltpu.make_async_copy(cot, slot(1, r, c), loc.at[3]),
         pltpu.make_async_copy(ci, CI.at[r], loc.at[4]),
     ]
     for cp in outs:
@@ -172,7 +175,7 @@
 
 
 def gather_all(tok, cot, wu, wd, ci):
-    full = jax.ShapeDtypeStruct((4, 8) + tok.shape, bf16)
+    full = jax.ShapeDtypeStruct((64, 4, 128, 128), bf16)
     return pl.pallas_call(
         gather_kernel,
         out_shape=(full, full, jax.ShapeDtypeStruct(wu.shape, bf16),
@@ -191,90 +194,112 @@
     )(tok, cot, wu, wd, ci)
 
 
-def row_kernel(ci, T, G, wu, wd, hid, gu, gd, xs, gs, ws):
-    i = pl.program_id(0)
-    row = lax.axis_index("row") * 4 + i
-    for k in range(16):
-        for a, (src, dst) in enumerate(((T, xs), (G, gs))):
-            b = ci[k // 4, a * 4 + k % 4, row]
-            lo = pl.multiple_of((b % 8) * 128, 128)
-            dst[:, k * 128:(k + 1) * 128] = src[:, b // 8, :, pl.ds(lo, 128)].reshape(512, 128)
-        ws[:, k * 128:(k + 1) * 128] = wd[k // 4, 0, k % 4]
-    pre = jnp.dot(xs[...], wu[...].reshape(2048, 128), preferred_element_type=f32)
-    back = lax.dot_general(gs[...], ws[...], (((1,), (1,)), ((), ())), preferred_element_type=f32)
-    sig = jax.nn.sigmoid(pre)
-    act = (pre * sig).astype(bf16)
-    slope = (back * sig * (1.0 + pre * (1.0 - sig))).astype(bf16)
-    hid[...] = act.reshape(4, 128, 128)
-    act_t = act.T
-    slope_t = slope.T
-    for k in range(0, 16, 4):
-        cols = slice(k * 128, (k + 4) * 128)
-        down = jnp.dot(act_t, gs[:, cols], preferred_element_type=f32)
-        up = jnp.dot(slope_t, xs[:, cols], preferred_element_type=f32)
-        for j in range(4):
-            gd[k // 4, 0, j] = down[:, j * 128:(j + 1) * 128].astype(bf16)
-            gu[k // 4, 0, j] = up[:, j * 128:(j + 1) * 128].T.astype(bf16)
+def row_kernel(ci, T, G, wu, wd, H, U, Dn, Tv, Gv, wuv, wdv, xs, gs, ws, hid, gu, gd,
+               load, send, recv, loc):
+    r, c, xn, yn, dg = place()
+    peers = (dg, xn, yn)
+    loads = []
+    for n, (src, dst) in enumerate(((T, Tv), (wu, wuv), (G, Gv), (wd, wdv))):
+        for g in range(4):
+            m = src.shape[0] // 4
+            part = pl.ds(g * m, m)
+            cp = pltpu.make_async_copy(src.at[part], dst.at[part], load.at[n, g])
+            cp.start()
+            loads.append(cp)
+    greet([(p, c) for p in peers])
+
+    def parts(i, p, src):
+        row = src * 4 + i
+        return (
+            (gu.at[i, p], U.at[row]),
+            (gd.at[i, p], Dn.at[row]),
+            (hid.at[i, p], H.at[:, pl.ds(pl.multiple_of(row * 128, 128), 128)]),
+        )
+
+    def puts(i):
+        cps = []
+        for n, p in enumerate(peers):
+            for j, (src, dst) in enumerate(parts(i, p, r)):
+                cps.append(pltpu.make_async_remote_copy(
+                    src_ref=src, dst_ref=dst, send_sem=send.at[i, n, j], recv_sem=recv.at[i, r, j],
+                    device_id=(p, c), device_id_type=MESH))
+        for j, (src, dst) in enumerate(parts(i, r, r)):
+            cps.append(pltpu.make_async_copy(src, dst, loc.at[i, j]))
+        return cps
+
+    def pick(i, a, src, dst):
+        for k in range(16):
+            b = ci[k // 4, a * 4 + k % 4, r * 4 + i]
+            dst[:, k * 128:(k + 1) * 128] = src[b].reshape(512, 128)
+
+    for cp in loads:
+        cp.wait()
+
+    @pl.loop(0, 4)
+    def _(i):
+        pick(i, 0, Tv, xs)
+        pre = jnp.dot(xs[...], wuv[:, i].reshape(2048, 128), preferred_element_type=f32)
+        pick(i, 1, Gv, gs)
+        for k in range(16):
+            ws[:, k * 128:(k + 1) * 128] = wdv[k // 4, i, k % 4]
+        back = lax.dot_general(gs[...], ws[...], (((1,), (1,)), ((), ())), preferred_element_type=f32)
+        sig = jax.nn.sigmoid(pre)
+        act = (pre * sig).astype(bf16)
+        slope = (back * sig * (1.0 + pre * (1.0 - sig))).astype(bf16)
+        hid[i] = act.reshape(4, 128, 128)
+        act_t = act.T
+        slope_t = slope.T
+        for k in range(0, 16, 4):
+            cols = slice(k * 128, (k + 4) * 128)
+            down = jnp.dot(act_t, gs[:, cols], preferred_element_type=f32)
+            up = jnp.dot(slope_t, xs[:, cols], preferred_element_type=f32)
+            for j in range(4):
+                gd[i, k // 4, j] = down[:, j * 128:(j + 1) * 128].astype(bf16)
+                gu[i, k // 4, j] = up[:, j * 128:(j + 1) * 128].T.astype(bf16)
+        for cp in puts(i):
+            cp.start()
+
+    @pl.loop(0, 4)
+    def _(i):
+        for n, p in enumerate(peers):
+            for j, (src, dst) in enumerate(parts(i, p, p)):
+                pltpu.make_async_remote_copy(
+                    src_ref=dst, dst_ref=dst, send_sem=send.at[i, n, j], recv_sem=recv.at[i, p, j],
+                    device_id=(p, c), device_id_type=MESH).wait_recv()
+        cps = puts(i)
+        for cp in cps[:9]:
+            cp.wait_send()
+        for cp in cps[9:]:
+            cp.wait()
 
 
 def rows_all(ci, T, G, wu, wd):
-    whole = pl.BlockSpec(T.shape, lambda i, s: (0, 0, 0, 0), pipeline_mode=pl.Buffered(1))
-    wspec = pl.BlockSpec((4, 1, 4, 128, 128), lambda i, s: (0, i, 0, 0, 0))
+    grad = jax.ShapeDtypeStruct((16, 4, 128, 128), bf16)
+    out = pltpu.VMEM((4, 4, 4, 128, 128), bf16)
     return pl.pallas_call(
         row_kernel,
-        out_shape=(jax.ShapeDtypeStruct((4, 128, 512), bf16),
-                   jax.ShapeDtypeStruct(wu.shape, bf16), jax.ShapeDtypeStruct(wd.shape, bf16)),
-        grid_spec=pltpu.PrefetchScalarGridSpec(
-            num_scalar_prefetch=1, grid=(4,),
-            in_specs=[whole, whole, wspec, wspec],
-            out_specs=(pl.BlockSpec((4, 128, 128), lambda i, s: (0, 0, i)), wspec, wspec),
-            scratch_shapes=[pltpu.VMEM((512, 2048), bf16), pltpu.VMEM((512, 2048), bf16),
-                            pltpu.VMEM((128, 2048), bf16)]),
-        compiler_params=pltpu.CompilerParams(vmem_limit_bytes=48 << 20),
+        out_shape=(jax.ShapeDtypeStruct((128, 2048), bf16), grad, grad),
+        in_specs=[pl.BlockSpec(memory_space=pltpu.SMEM), ANY, ANY, ANY, ANY],
+        out_specs=(ANY,) * 3,
+        scratch_shapes=[
+            pltpu.VMEM(T.shape, bf16), pltpu.VMEM(G.shape, bf16),
+            pltpu.VMEM(wu.shape, bf16), pltpu.VMEM(wd.shape, bf16),
+            pltpu.VMEM((512, 2048), bf16), pltpu.VMEM((512, 2048), bf16),
+            pltpu.VMEM((128, 2048), bf16),
+            pltpu.VMEM((4, 4, 128, 128), bf16), out, out,
+            pltpu.SemaphoreType.DMA((4, 4)),
+            pltpu.SemaphoreType.DMA((4, 3, 3)),
+            pltpu.SemaphoreType.DMA((4, 4, 3)),
+            pltpu.SemaphoreType.DMA((4, 3)),
+        ],
+        compiler_params=pltpu.CompilerParams(
+            collective_id=1, has_side_effects=True, vmem_limit_bytes=56 << 20),
         name="rows_all",
     )(ci, T, G, wu, wd)
 
 
-def scatter_kernel(hid, gu, gd, H, U, Dn, send, recv, loc):
-    r, c, xn, yn, dg = place()
-    peers = (dg, xn, yn)
-    greet([(p, c) for p in peers])
-    put = Puts(send)
-
-    def dests(rr):
-        return (U.at[pl.ds(rr * 4, 4)], Dn.at[pl.ds(rr * 4, 4)],
-                H.at[:, pl.ds(pl.multiple_of(rr * 512, 512), 512)])
-
-    mine = dests(r)
-    for p in peers:
-        for j, s in enumerate((gu, gd, hid)):
-            put(s.at[p], mine[j], recv.at[j, r], (p, c))
-    outs = [pltpu.make_async_copy(s.at[r], mine[j], loc.at[j]) for j, s in enumerate((gu, gd, hid))]
-    for cp in outs:
-        cp.start()
-    for p in peers:
-        for j, t in enumerate(dests(p)):
-            put.got(t, recv.at[j, p], (p, c))
-    for cp in outs:
-        cp.wait()
-    put.drain()
-
-
-def scatter_all(hid, gu, gd):
-    grad = jax.ShapeDtypeStruct((16,) + gu.shape[2:], bf16)
-    return pl.pallas_call(
-        scatter_kernel,
-        out_shape=(jax.ShapeDtypeStruct((128, 2048), bf16), grad, grad),
-        in_specs=[VM] * 3,
-        out_specs=(ANY,) * 3,
-        scratch_shapes=[
-            pltpu.SemaphoreType.DMA((9,)),
-            pltpu.SemaphoreType.DMA((3, 4)),
-            pltpu.SemaphoreType.DMA((3,)),
-        ],
-        compiler_params=pltpu.CompilerParams(collective_id=1, has_side_effects=True),
-        name="scatter_all",
-    )(hid, gu, gd)
+def blocked(rows):
+    return rows.reshape(128, 8, 128).transpose(1, 0, 2)
 
 
 def per_row(tokens, cotangent, up_blocks, up_cols, down_blocks, down_cols):
@@ -282,9 +307,8 @@
     wd = down_blocks.reshape(4, 4, 4, 128, 128)
     ci = jnp.concatenate([up_cols.T, down_cols.T], axis=0)
     ci = jnp.pad(ci, ((0, 0), (0, 112)))
-    T, G, WU, WD, CI = gather_all(tokens, cotangent, wu, wd, ci)
-    hid, gu, gd = rows_all(CI, T, G, WU, WD)
-    return scatter_all(hid, gu, gd)
+    T, G, WU, WD, CI = gather_all(blocked(tokens), blocked(cotangent), wu, wd, ci)
+    return rows_all(CI, T, G, WU, WD)
 
 
 def per_device(tokens, cotangent, up_blocks, up_cols, down_blocks, down_cols):

time: 187 us -> 176 us (0.941)
  Pallas kernels: 174 us -> 163 us
    pallas_call x2 -> x1, Pallas kernels: 74.5 us -> 63.6 us  [rows_all(): pl.pallas_call(row_kernel, out_shape=(jax.ShapeDtypeStruct((128, 2048), b...]
    unnamed x13 -> x7, local copies, waits for them, and re-layouts: 10.6 us -> 8.74 us
where the time goes in v3:
time: 176 us
  Pallas kernels  163 us (93%)
  local copies, waits for them, and re-layouts  11.1 us (6%)
    pallas_call x1, Pallas kernels, gather_all(): pl.pallas_call(gather_kernel, out_shape=(full, full, jax.ShapeDtypeStruct...  99.6 us
    pallas_call x1, Pallas kernels, rows_all(): pl.pallas_call(row_kernel, out_shape=(jax.ShapeDtypeStruct((128, 2048), b...  63.6 us
    unnamed x7, local copies, waits for them, and re-layouts  8.74 us

profile of v3, /device:TPU:0, one launch (start us, length us, event | category | flops | bytes accessed | tf_op | source)
XLA Modules:
  0.0 175.7 jit_solution(1087298588457984456)
XLA Ops:
  0.6 0.7 pad_add_fusion
  1.3 0.6 pad.4.ci
  1.9 1.1 copy.9
  3.1 0.9 copy.10
  3.9 1.1 copy.11
  5.0 0.9 copy.12
  5.9 99.6 %gather_all.1 = (bf16[64,4,128,128]{3,2,1,0:T(8,128)(2,1)}, bf16[64,4,128,128]{3,2,1,0:T(8,128)(2,1)}, bf16[4,4,4,128,128]{4,3,2,1,0:T(8,128)(2,1)}, bf16[4,4,4,128,128]{4,3,2,1,0:T(8,128)(2,1)}, s32[4,8,128]{2,1,0:T(8,128)}) custom-call(bf16[8,128,128]{2,1,0:T(8,128)(2,1)} %bitcast.12, bf16[8,128,128]{2,1,0:T(8,128)(2,1)} %bitcast.13, ...), custom_call_target="tpu_custom_call" | custom-call | tf_op jit(solution)/shard_map/gather_all/pallas_call | solution.py:179
  105.5 63.6 %rows_all.1 = (bf16[128,2048]{1,0:T(8,128)(2,1)}, bf16[16,4,128,128]{3,2,1,0:T(8,128)(2,1)}, bf16[16,4,128,128]{3,2,1,0:T(8,128)(2,1)}) custom-call(s32[4,8,128]{2,1,0:T(8,128)} %get-tuple-element.8.ci, bf16[64,4,128,128]{3,2,1,0:T(8,128)(2,1)} %get-tuple-element.9.T, bf16[64,4,128,128]{3,2,1,0:T(8,128)(2,1)} %get-tuple-element.10.G, ...), custom_call_target="tpu_custom_call" | custom-call | tf_op jit(solution)/shard_map/rows_all/pallas_call | solution.py:279
  169.2 1.9 %copy.16 = bf16[128,2048]{1,0:T(8,128)(2,1)} copy(bf16[128,2048]{1,0:T(8,128)(2,1)} %get-tuple-element.16) | data formatting | bytes 1048576
  171.0 0.0 copy-start
  171.0 3.3 %copy.17 = bf16[16,4,128,128]{3,2,1,0:T(8,128)(2,1)} copy(bf16[16,4,128,128]{3,2,1,0:T(8,128)(2,1)} %get-tuple-element.17) | data formatting | bytes 4194304
  174.4 0.0 copy-done
  174.4 1.3 copy.18
Async XLA Ops:
  171.0 3.3 %copy-start = (bf16[16,4,128,128]{3,2,1,0:T(8,128)(2,1)S(1)}, bf16[16,4,128,128]{3,2,1,0:T(8,128)(2,1)}, u32[]{:S(2)}) copy-start(bf16[16,4,128,128]{3,2,1,0:T(8,128)(2,1)} %get-tuple-element.18) | copy-start | bytes 6291460

commit v4 on v3

--- a/solution.py
+++ b/solution.py
@@ -9,7 +9,6 @@
 
 MESH = pl.DeviceIdType.MESH
 ANY = pl.BlockSpec(memory_space=pl.ANY)
-VM = pl.BlockSpec(memory_space=pltpu.VMEM)
 f32 = jnp.float32
 bf16 = jnp.bfloat16
 
@@ -57,7 +56,8 @@
     pl.semaphore_wait(sem, len(devs))
 
 
-def gather_kernel(tok, cot, wu, wd, ci, T, G, WU, WD, CI, own, send, recv, wrecv, loc):
+def layer_kernel(tokens, cotangent, wu, wd, ci, H, U, Dn, tok, cot, T, G, WU, WD, CI, cols,
+                 xs, gs, ws, hid, gu, gd, send, recv, wrecv, loc, gsend, grecv, gloc):
     r, c, xn, yn, dg = place()
     z, q = c // 2, c % 2
     pc = c + 1 - 2 * q
@@ -66,7 +66,6 @@
     zcs = [((z + d) % 4) * 2 + q for d in range(4)]
     X, Y, D, Q = (xn, c), (yn, c), (dg, c), (r, pc)
     rows = (r, xn, yn, dg)
-    greet([(r, zc) for zc in zcs[1:]] + [X, Y, D, Q])
     put = Puts(send)
 
     def slot(a, rr, cc):
@@ -79,13 +78,21 @@
     def got(a, rr, cc):
         put.got(slot(a, rr, cc), recv.at[a, rr, cc], Q)
 
-    ins = [pltpu.make_async_copy(w.at[r], own.at[j], loc.at[j]) for j, w in enumerate((wu, wd))]
+    ins = []
+    for a, (src, dst) in enumerate(((cotangent, cot), (tokens, tok))):
+        for j in range(8):
+            cp = pltpu.make_async_copy(src.at[:, j * 128:(j + 1) * 128], dst.at[j], loc.at[a * 8 + j])
+            cp.start()
+            ins.append(cp)
+    greet([(r, zc) for zc in zcs[1:]] + [X, Y, D, Q])
     for cp in ins:
-        cp.start()
+        cp.wait()
     outs = [
-        pltpu.make_async_copy(tok, slot(0, r, c), loc.at[2]),
-        pltpu.make_async_copy(cot, slot(1, r, c), loc.at[3]),
-        pltpu.make_async_copy(ci, CI.at[r], loc.at[4]),
+        pltpu.make_async_copy(tok, slot(0, r, c), loc.at[16]),
+        pltpu.make_async_copy(cot, slot(1, r, c), loc.at[17]),
+        pltpu.make_async_copy(ci, CI.at[r], loc.at[18]),
+        pltpu.make_async_copy(wu.at[r], WU.at[r], loc.at[19]),
+        pltpu.make_async_copy(wd.at[r], WD.at[r], loc.at[20]),
     ]
     for cp in outs:
         cp.start()
@@ -94,9 +101,17 @@
         fwd(1, rr, c, (r, c + 2), src, z < 3)
         fwd(1, rr, c, (r, c - 2), src, z > 0)
 
-    def weights(j):
-        for peer in (dg, xn, yn):
-            put((wu, wd)[j].at[peer], (WU, WD)[j].at[r], wrecv.at[j, r], (peer, c))
+    def weights(h):
+        half = pl.ds(2 * h, 2)
+        for j in range(2):
+            for peer in (dg, xn, yn):
+                put((wu, wd)[j].at[peer, half], (WU, WD)[j].at[r, half], wrecv.at[2 * h + j, r], (peer, c))
+
+    def weights_in(h):
+        half = pl.ds(2 * h, 2)
+        for j in range(2):
+            for peer in (dg, xn, yn):
+                put.got((WU, WD)[j].at[peer, half], wrecv.at[2 * h + j, peer], (peer, c))
 
     fwd(1, r, c, X, cot)
     fwd(1, r, c, Y, cot)
@@ -108,7 +123,7 @@
     fwd(0, r, c, Q, tok)
     fwd(1, r, c, Q, cot)
     for peer in (dg, xn, yn):
-        put(ci, CI.at[r], wrecv.at[2, r], (peer, c))
+        put(ci, CI.at[r], wrecv.at[4, r], (peer, c))
     got(1, first, c)
     fwd(1, first, c, (second, c))
     got(1, second, c)
@@ -119,12 +134,6 @@
     got(1, dg, c)
     along(dg)
     fwd(1, dg, c, Q)
-    for j, cp in enumerate(ins):
-        cp.wait()
-        cp = pltpu.make_async_copy(own.at[j], (WU, WD)[j].at[r], loc.at[5 + j])
-        cp.start()
-        outs.append(cp)
-
     def relay(d):
         got(0, first, zcs[d])
         fwd(0, first, zcs[d], (second, c))
@@ -162,51 +171,19 @@
             got(0, rr, zcs[d])
             fwd(0, rr, zcs[d], Q)
     onward(3)
-    for j, t in enumerate((WU, WD, CI)):
-        for peer in (dg, xn, yn):
-            put.got(t.at[peer], wrecv.at[j, peer], (peer, c))
+    for peer in (dg, xn, yn):
+        put.got(CI.at[peer], wrecv.at[4, peer], (peer, c))
+    for cp in outs:
+        cp.wait()
+    table = pltpu.make_async_copy(CI, cols, loc.at[21])
+    table.start()
+    weights_in(0)
+    table.wait()
     for a in range(2):
         for d in range(4):
             for rr in rows:
                 got(a, rr, ((z + d) % 4) * 2 + 1 - q)
-    for cp in outs:
-        cp.wait()
-    put.drain()
-
-
-def gather_all(tok, cot, wu, wd, ci):
-    full = jax.ShapeDtypeStruct((64, 4, 128, 128), bf16)
-    return pl.pallas_call(
-        gather_kernel,
-        out_shape=(full, full, jax.ShapeDtypeStruct(wu.shape, bf16),
-                   jax.ShapeDtypeStruct(wd.shape, bf16), jax.ShapeDtypeStruct((4,) + ci.shape, ci.dtype)),
-        in_specs=[VM, VM, ANY, ANY, ANY],
-        out_specs=(ANY,) * 5,
-        scratch_shapes=[
-            pltpu.VMEM((2,) + wu.shape[1:], bf16),
-            pltpu.SemaphoreType.DMA((96,)),
-            pltpu.SemaphoreType.DMA((2, 4, 8)),
-            pltpu.SemaphoreType.DMA((3, 4)),
-            pltpu.SemaphoreType.DMA((7,)),
-        ],
-        compiler_params=pltpu.CompilerParams(collective_id=0, has_side_effects=True),
-        name="gather_all",
-    )(tok, cot, wu, wd, ci)
-
-
-def row_kernel(ci, T, G, wu, wd, H, U, Dn, Tv, Gv, wuv, wdv, xs, gs, ws, hid, gu, gd,
-               load, send, recv, loc):
-    r, c, xn, yn, dg = place()
     peers = (dg, xn, yn)
-    loads = []
-    for n, (src, dst) in enumerate(((T, Tv), (wu, wuv), (G, Gv), (wd, wdv))):
-        for g in range(4):
-            m = src.shape[0] // 4
-            part = pl.ds(g * m, m)
-            cp = pltpu.make_async_copy(src.at[part], dst.at[part], load.at[n, g])
-            cp.start()
-            loads.append(cp)
-    greet([(p, c) for p in peers])
 
     def parts(i, p, src):
         row = src * 4 + i
@@ -221,27 +198,25 @@
         for n, p in enumerate(peers):
             for j, (src, dst) in enumerate(parts(i, p, r)):
                 cps.append(pltpu.make_async_remote_copy(
-                    src_ref=src, dst_ref=dst, send_sem=send.at[i, n, j], recv_sem=recv.at[i, r, j],
+                    src_ref=src, dst_ref=dst, send_sem=gsend.at[i, n, j], recv_sem=grecv.at[i, r, j],
                     device_id=(p, c), device_id_type=MESH))
         for j, (src, dst) in enumerate(parts(i, r, r)):
-            cps.append(pltpu.make_async_copy(src, dst, loc.at[i, j]))
+            cps.append(pltpu.make_async_copy(src, dst, gloc.at[i, j]))
         return cps
 
     def pick(i, a, src, dst):
         for k in range(16):
-            b = ci[k // 4, a * 4 + k % 4, r * 4 + i]
+            b = cols[k // 4, a * 4 + k % 4, r * 4 + i]
             dst[:, k * 128:(k + 1) * 128] = src[b].reshape(512, 128)
-
-    for cp in loads:
-        cp.wait()
 
     @pl.loop(0, 4)
     def _(i):
-        pick(i, 0, Tv, xs)
-        pre = jnp.dot(xs[...], wuv[:, i].reshape(2048, 128), preferred_element_type=f32)
-        pick(i, 1, Gv, gs)
+        pl.when(i == 2)(functools.partial(weights_in, 1))
+        pick(i, 0, T, xs)
+        pre = jnp.dot(xs[...], WU[:, i].reshape(2048, 128), preferred_element_type=f32)
+        pick(i, 1, G, gs)
         for k in range(16):
-            ws[:, k * 128:(k + 1) * 128] = wdv[k // 4, i, k % 4]
+            ws[:, k * 128:(k + 1) * 128] = WD[k // 4, i, k % 4]
         back = lax.dot_general(gs[...], ws[...], (((1,), (1,)), ((), ())), preferred_element_type=f32)
         sig = jax.nn.sigmoid(pre)
         act = (pre * sig).astype(bf16)
@@ -264,7 +239,7 @@
         for n, p in enumerate(peers):
             for j, (src, dst) in enumerate(parts(i, p, p)):
                 pltpu.make_async_remote_copy(
-                    src_ref=dst, dst_ref=dst, send_sem=send.at[i, n, j], recv_sem=recv.at[i, p, j],
+                    src_ref=dst, dst_ref=dst, send_sem=gsend.at[i, n, j], recv_sem=grecv.at[i, p, j],
                     device_id=(p, c), device_id_type=MESH).wait_recv()
         cps = puts(i)
         for cp in cps[:9]:
@@ -273,33 +248,37 @@
             cp.wait()
 
 
-def rows_all(ci, T, G, wu, wd):
+    put.drain()
+
+
+def layer(tokens, cotangent, wu, wd, ci):
     grad = jax.ShapeDtypeStruct((16, 4, 128, 128), bf16)
-    out = pltpu.VMEM((4, 4, 4, 128, 128), bf16)
+    unit = pltpu.VMEM((8, 128, 128), bf16)
+    full = pltpu.VMEM((64, 4, 128, 128), bf16)
+    weight = pltpu.VMEM(wu.shape, bf16)
+    picked = pltpu.VMEM((512, 2048), bf16)
     return pl.pallas_call(
-        row_kernel,
+        layer_kernel,
         out_shape=(jax.ShapeDtypeStruct((128, 2048), bf16), grad, grad),
-        in_specs=[pl.BlockSpec(memory_space=pltpu.SMEM), ANY, ANY, ANY, ANY],
+        in_specs=[ANY] * 5,
         out_specs=(ANY,) * 3,
         scratch_shapes=[
-            pltpu.VMEM(T.shape, bf16), pltpu.VMEM(G.shape, bf16),
-            pltpu.VMEM(wu.shape, bf16), pltpu.VMEM(wd.shape, bf16),
-            pltpu.VMEM((512, 2048), bf16), pltpu.VMEM((512, 2048), bf16),
-            pltpu.VMEM((128, 2048), bf16),
-            pltpu.VMEM((4, 4, 128, 128), bf16), out, out,
-            pltpu.SemaphoreType.DMA((4, 4)),
+            unit, unit, full, full, weight, weight,
+            pltpu.VMEM((4, 8, 128), jnp.int32), pltpu.SMEM((4, 8, 128), jnp.int32),
+            picked, picked, pltpu.VMEM((128, 2048), bf16),
+            pltpu.VMEM((4, 4, 128, 128), bf16), weight, weight,
+            pltpu.SemaphoreType.DMA((104,)),
+            pltpu.SemaphoreType.DMA((2, 4, 8)),
+            pltpu.SemaphoreType.DMA((5, 4)),
+            pltpu.SemaphoreType.DMA((22,)),
             pltpu.SemaphoreType.DMA((4, 3, 3)),
             pltpu.SemaphoreType.DMA((4, 4, 3)),
             pltpu.SemaphoreType.DMA((4, 3)),
         ],
         compiler_params=pltpu.CompilerParams(
-            collective_id=1, has_side_effects=True, vmem_limit_bytes=56 << 20),
-        name="rows_all",
-    )(ci, T, G, wu, wd)
-
-
-def blocked(rows):
-    return rows.reshape(128, 8, 128).transpose(1, 0, 2)
+            collective_id=0, has_side_effects=True, vmem_limit_bytes=56 << 20),
+        name="layer",
+    )(tokens, cotangent, wu, wd, ci)
 
 
 def per_row(tokens, cotangent, up_blocks, up_cols, down_blocks, down_cols):
@@ -307,8 +286,7 @@
     wd = down_blocks.reshape(4, 4, 4, 128, 128)
     ci = jnp.concatenate([up_cols.T, down_cols.T], axis=0)
     ci = jnp.pad(ci, ((0, 0), (0, 112)))
-    T, G, WU, WD, CI = gather_all(blocked(tokens), blocked(cotangent), wu, wd, ci)
-    return rows_all(CI, T, G, WU, WD)
+    return layer(tokens, cotangent, wu, wd, ci)
 
 
 def per_device(tokens, cotangent, up_blocks, up_cols, down_blocks, down_cols):

time: 176 us -> 163 us (0.926)
  Pallas kernels: 163 us -> 154 us
  local copies, waits for them, and re-layouts: 11.1 us -> 7.11 us
    pallas_call x2 -> x1, Pallas kernels: 163 us -> 154 us  [layer(): pl.pallas_call(layer_kernel, out_shape=(jax.ShapeDtypeStruct((128, 2048),...]
    unnamed x7 -> x5, local copies, waits for them, and re-layouts: 8.74 us -> 6.51 us
where the time goes in v4:
time: 163 us; the launch traced here: 162 us
  Pallas kernels  154 us (94%)
  local copies, waits for them, and re-layouts  7.11 us (4%)
    pallas_call x1, Pallas kernels, layer(): pl.pallas_call(layer_kernel, out_shape=(jax.ShapeDtypeStruct((128, 2048),...  154 us
    unnamed x5, local copies, waits for them, and re-layouts  6.51 us

profile of v4, /device:TPU:0, one launch (start us, length us, event | category | flops | bytes accessed | tf_op | source)
XLA Modules:
  0.0 162.4 jit_solution(2878418889078805800)
XLA Ops:
  0.6 0.7 pad_add_fusion
  1.3 0.6 pad.4.ci
  1.9 153.9 %layer.1 = (bf16[128,2048]{1,0:T(8,128)(2,1)}, bf16[16,4,128,128]{3,2,1,0:T(8,128)(2,1)}, bf16[16,4,128,128]{3,2,1,0:T(8,128)(2,1)}) custom-call(bf16[128,1024]{1,0:T(8,128)(2,1)} %tokens.1, bf16[128,1024]{1,0:T(8,128)(2,1)} %cotangent.1, bf16[4,4,4,128,128]{4,3,2,1,0:T(8,128)(2,1)} %bitcast.4, bf16[4,4,4,128,128]{4,3,2,1,0:T(8,128)(2,1)} %bitcast.5, ...), custom_call_target="tpu_custom_call" | custom-call | tf_op jit(solution)/shard_map/layer/pallas_call | solution.py:260
  155.9 1.9 %copy.12 = bf16[128,2048]{1,0:T(8,128)(2,1)} copy(bf16[128,2048]{1,0:T(8,128)(2,1)} %get-tuple-element.6) | data formatting | bytes 1048576
  157.8 0.0 copy-start
  157.8 3.3 %copy.13 = bf16[16,4,128,128]{3,2,1,0:T(8,128)(2,1)} copy(bf16[16,4,128,128]{3,2,1,0:T(8,128)(2,1)} %get-tuple-element.7) | data formatting | bytes 4194304
  161.1 0.0 copy-done
  161.1 1.3 copy.14
Async XLA Ops:
  157.8 3.3 %copy-start = (bf16[16,4,128,128]{3,2,1,0:T(8,128)(2,1)S(1)}, bf16[16,4,128,128]{3,2,1,0:T(8,128)(2,1)}, u32[]{:S(2)}) copy-start(bf16[16,4,128,128]{3,2,1,0:T(8,128)(2,1)} %get-tuple-element.8) | copy-start | bytes 6291460

commit v5 on v4

--- a/solution.py
+++ b/solution.py
@@ -281,12 +281,41 @@
     )(tokens, cotangent, wu, wd, ci)
 
 
+def settle_kernel(h, u, d, H, U, Dn, vh, vu, vd, si, so):
+    pieces = []
+    for n, (src, via, dst) in enumerate(((u, vu, U), (d, vd, Dn), (h, vh, H))):
+        m = src.shape[0] // 4
+        for g in range(4):
+            part = pl.ds(g * m, m)
+            a = pltpu.make_async_copy(src.at[part], via.at[part], si.at[n, g])
+            a.start()
+            pieces.append((a, pltpu.make_async_copy(via.at[part], dst.at[part], so.at[n, g])))
+    for a, z in pieces:
+        a.wait()
+        z.start()
+    for _, z in pieces:
+        z.wait()
+
+
+def settle(*outs):
+    return pl.pallas_call(
+        settle_kernel,
+        out_shape=tuple(jax.ShapeDtypeStruct(o.shape, o.dtype) for o in outs),
+        in_specs=[ANY] * 3,
+        out_specs=(ANY,) * 3,
+        scratch_shapes=[pltpu.VMEM(o.shape, o.dtype) for o in outs]
+        + [pltpu.SemaphoreType.DMA((3, 4))] * 2,
+        compiler_params=pltpu.CompilerParams(vmem_limit_bytes=56 << 20),
+        name="settle",
+    )(*outs)
+
+
 def per_row(tokens, cotangent, up_blocks, up_cols, down_blocks, down_cols):
     wu = up_blocks.reshape(4, 4, 4, 128, 128)
     wd = down_blocks.reshape(4, 4, 4, 128, 128)
     ci = jnp.concatenate([up_cols.T, down_cols.T], axis=0)
     ci = jnp.pad(ci, ((0, 0), (0, 112)))
-    return layer(tokens, cotangent, wu, wd, ci)
+    return settle(*layer(tokens, cotangent, wu, wd, ci))
 
 
 def per_device(tokens, cotangent, up_blocks, up_cols, down_blocks, down_cols):

time: 163 us -> 160 us (0.982)
  local copies, waits for them, and re-layouts: 7.11 us -> 0.6 us
  Pallas kernels: 154 us -> 158 us
    unnamed x5 -> x0, local copies, waits for them, and re-layouts: 6.51 us -> none
    pallas_call x0 -> x1, Pallas kernels: none -> 4.05 us  [settle(): pl.pallas_call(settle_kernel, out_shape=tuple((jax.ShapeDtypeStruct(o.sha...]
where the time goes in v5:
time: 160 us
  Pallas kernels  158 us (99%)
    pallas_call x1, Pallas kernels, layer(): pl.pallas_call(layer_kernel, out_shape=(jax.ShapeDtypeStruct((128, 2048),...  154 us
    pallas_call x1, Pallas kernels, settle(): pl.pallas_call(settle_kernel, out_shape=tuple((jax.ShapeDtypeStruct(o.sha...  4.05 us

profile of v5, /device:TPU:0, one launch (start us, length us, event | category | flops | bytes accessed | tf_op | source)
XLA Modules:
  0.0 159.9 jit_solution(13201624149461039849)
XLA Ops:
  0.6 0.7 pad_add_fusion
  1.3 0.6 pad.4.ci
  1.9 153.9 %layer.1 = (bf16[128,2048]{1,0:T(8,128)(2,1)}, bf16[16,4,128,128]{3,2,1,0:T(8,128)(2,1)}, bf16[16,4,128,128]{3,2,1,0:T(8,128)(2,1)}) custom-call(bf16[128,1024]{1,0:T(8,128)(2,1)} %tokens.1, bf16[128,1024]{1,0:T(8,128)(2,1)} %cotangent.1, bf16[4,4,4,128,128]{4,3,2,1,0:T(8,128)(2,1)} %bitcast.4, bf16[4,4,4,128,128]{4,3,2,1,0:T(8,128)(2,1)} %bitcast.5, ...), custom_call_target="tpu_custom_call" | custom-call | tf_op jit(solution)/shard_map/layer/pallas_call | solution.py:260
  155.9 4.0 %settle.1 = (bf16[128,2048]{1,0:T(8,128)(2,1)}, bf16[16,4,128,128]{3,2,1,0:T(8,128)(2,1)}, bf16[16,4,128,128]{3,2,1,0:T(8,128)(2,1)}) custom-call(bf16[128,2048]{1,0:T(8,128)(2,1)} %get-tuple-element.6.h, bf16[16,4,128,128]{3,2,1,0:T(8,128)(2,1)} %get-tuple-element.7.u, bf16[16,4,128,128]{3,2,1,0:T(8,128)(2,1)} %get-tuple-element.8.d), custom_call_target="tpu_custom_call" | custom-call | tf_op jit(solution)/shard_map/settle/pallas_call | solution.py:301
